TPU v7x, 128 devices: a whole 4x4x4 slice. The times are simulated.
128 devices in a mesh: lat: 16 (over y, z), lon: 8 (over x, core).
Axes of the slice: x: 4, y: 4, z: 4, core: 2. Of those that a mesh axis runs over, the one named last changes fastest.
Arguments:
- inputs: bfloat16 [640, 1440, 256], P('lat', 'lon'), may hold values from -6 to 6
- w_enc: bfloat16 [3, 3, 256, 256], replicated, may hold values from -0.125 to 0.125
- w_proj: bfloat16 [256, 128], replicated, may hold values from -0.375 to 0.375
- film_scale: float32 [720, 128], replicated, may hold values from -3 to 3
- film_shift: float32 [720, 128], replicated, may hold values from -3 to 3
- lead_ids: int32 [16], replicated, may hold values from 0 to 719
- w_head: bfloat16 [3, 3, 128, 128], replicated, may hold values from -0.1875 to 0.1875
- zonal_mix: bfloat16 [720, 720], replicated, may hold values from -0.21875 to 0.21875
Outputs:
- forecast: bfloat16 [16, 320, 720, 128], P('lon', 'lat')
Inputs may be any that keep to these rules, and one draw needn't show every extreme that they name: `lead_ids`: rows of the tables; repeats may occur.
All inputs are finite; a program needn't handle non-finite values.
Results may differ from a plain program's by a relative error of at most 0.015.
Values may be sent and summed in bfloat16 or wider, within the bound.
A program may use at most 128 MiB of HBM per device.

v0:
```python
import jax
import jax.numpy as jnp
from jax import lax
from jax.sharding import PartitionSpec as P

LEAD_DEV = 2


def extended(x, sides, width, wrap):
    for axis, dim in sides:
        devices, length = (lax.axis_size(axis), x.shape[dim])
        up = [(i, (i + 1) % devices) for i in range(devices if wrap else devices - 1)]
        down = [(j, i) for i, j in up]
        last = lax.slice_in_dim(x, length - width, length, axis=dim)
        initial = lax.slice_in_dim(x, 0, width, axis=dim)
        before = lax.ppermute(last, axis, up)
        after = lax.ppermute(initial, axis, down)
        x = jnp.concatenate([before, x, after], axis=dim)
    return x


def conv_three(padded, weight):
    batched = padded if padded.ndim == 4 else padded[None]
    result = lax.conv_general_dilated(
        batched,
        weight,
        (1, 1),
        "VALID",
        dimension_numbers=("NHWC", "HWIO", "NHWC"),
        preferred_element_type=jnp.float32,
    )
    return result if padded.ndim == 4 else result[0]


def pool_pairs(field):
    summed = lax.reduce_window(
        field, jnp.array(0, field.dtype), lax.add, (2, 2, 1), (2, 2, 1), "VALID"
    )
    return summed * 0.25


def wrap_columns(field):
    return jnp.concatenate([field[..., -1:, :], field, field[..., :1, :]], axis=-2)


def modulate(projected, scales, shifts):
    widened = projected.astype(jnp.float32)[None]
    return (widened * (1.0 + scales[:, None, None, :]) + shifts[:, None, None, :]).astype(
        jnp.bfloat16
    )


def shards(inputs, w_enc, w_proj, film_scale, film_shift, lead_ids, w_head, zonal_mix):
    lat_rows, lon_cols, channels = inputs.shape
    with_rows = extended(inputs, (("lat", 0),), 1, False)
    padded = extended(with_rows, (("lon", 1),), 1, True)
    encoded = jax.nn.gelu(conv_three(padded, w_enc))
    pooled = pool_pairs(encoded).astype(jnp.bfloat16)
    head_width = w_proj.shape[1]
    lon_group = lax.axis_index("lon")
    my_rows = lax.dynamic_slice_in_dim(lead_ids, lon_group * LEAD_DEV, LEAD_DEV)
    flat = jnp.dot(pooled.reshape(-1, channels), w_proj, preferred_element_type=jnp.float32)
    band_proj = lax.all_gather(
        flat.astype(jnp.bfloat16).reshape(pooled.shape[0], pooled.shape[1], head_width),
        "lon",
        axis=1,
        tiled=True,
    )
    onehot = (my_rows[:, None] == jnp.arange(film_scale.shape[0], dtype=jnp.int32)[None, :]).astype(
        jnp.float32
    )
    scales = jnp.dot(onehot, film_scale, precision=lax.Precision.HIGHEST)
    shifts = jnp.dot(onehot, film_shift, precision=lax.Precision.HIGHEST)
    scales, shifts = (scales, shifts)
    with_band = None
    modulated = modulate(band_proj, scales, shifts)
    with_band = extended(modulated, (("lat", 1),), 1, False)
    padded_head = wrap_columns(with_band)
    hidden = jax.nn.gelu(conv_three(padded_head, w_head)).astype(jnp.bfloat16)
    mixed = jnp.einsum("ij,bajc->baic", zonal_mix, hidden, preferred_element_type=jnp.float32)
    return (modulated.astype(jnp.float32) + mixed).astype(jnp.bfloat16)


def solution(mesh):
    in_specs = (P("lat", "lon", None), P(), P(), P(), P(), P(), P(), P())
    out_specs = P("lon", "lat", None, None)
    return jax.shard_map(shards, mesh=mesh, in_specs=in_specs, out_specs=out_specs, check_vma=False)
```

profile of v0, /device:TPU:96, one launch (start us, length us, event | category | flops | bytes accessed | tf_op | source)
XLA Modules:
  0.0 219.7 jit_solution(3243540371353144879)
XLA Ops:
  6.5 1.8 fusion.43
  8.4 2.4 %collective-permute-start.1 = (bf16[1,180,256]{2,1,0:T(8,128)(2,1)S(1)}, bf16[1,180,256]{2,1,0:T(8,128)(2,1)S(1)}, u32[]{:S(2)}, u32[]{:S(2)}) collective-permute-start(bf16[1,180,256]{2,1,0:T(8,128)(2,1)S(1)} %copy.64), channel_id=1, source_target_pairs={{8,0},{16,8},{24,16},{32,24},{40,32},{48,40},{56,48},{64,56},{72,6... | collective-permute-start | bytes 276488 | tf_op jit(solution)/shard_map/ppermute | solution.py:17
  10.8 5.6 %collective-permute-start = (bf16[1,180,256]{2,1,0:T(8,128)(2,1)S(1)}, bf16[1,180,256]{2,1,0:T(8,128)(2,1)S(1)}, u32[]{:S(2)}, u32[]{:S(2)}) collective-permute-start(bf16[1,180,256]{2,1,0:T(8,128)(2,1)S(1)} %copy.63), channel_id=1, source_target_pairs={{0,8},{8,16},{16,24},{24,32},{32,40},{40,48},{48,56},{56,64},{64,7... | collective-permute-start | bytes 276488 | tf_op jit(solution)/shard_map/ppermute | solution.py:16
  16.5 0.6 collective-permute-done.1
  17.1 0.1 copy.46
  17.2 1.4 collective-permute-done
  18.6 0.1 copy.45
  18.8 0.8 pad_maximum_fusion.6
  19.5 0.0 collective-permute-start.2
  19.6 2.9 %collective-permute-start.3 = (bf16[42,1,256]{2,0,1:T(8,128)(2,1)S(1)}, bf16[42,1,256]{2,0,1:T(8,128)(2,1)S(1)}, u32[]{:S(2)}, u32[]{:S(2)}) collective-permute-start(bf16[42,1,256]{2,0,1:T(8,128)(2,1)S(1)} %get-tuple-element.8), channel_id=1, source_target_pairs={{1,0},{2,1},{3,2},{4,3},{5,4},{6,5},{7,6},{0,7},{9,8},{10,9},{11,1... | collective-permute-start | bytes 64520 | tf_op jit(solution)/shard_map/ppermute | solution.py:17
  22.5 1.5 collective-permute-done.2
  24.0 0.0 collective-permute-done.3
  24.0 3.2 %maximum_bitcast_fusion = bf16[42,1,182,256]{3,0,2,1:T(8,128)(2,1)S(1)} fusion(bf16[42,1,256]{2,0,1:T(8,128)(2,1)S(1)} %collective-permute-done.3, bf16[1,180,256]{2,0,1:T(2,128)(2,1)S(1)} %copy.46, bf16[40,180,256]{2,0,1:T(8,128)(2,1)S(1)} %copy-done.2, bf16[1,180,256]{2,0,1:T(2,128)(2,1)S(1)} %copy.45, bf16[42,1,256]{2,0,1:T(8,128)(2,1)S(1)} %collective-permute-done.2), kind=kLoop, calls=%fused_computation.37 | loop fusion | flops 19568640 | bytes 7827456 | tf_op jit(solution)/shard_map/broadcast_in_dim | solution.py:23
  27.2 0.4 pad
  27.6 1.5 copy.49
  29.1 0.1 slice.36
  29.2 9.5 %broadcast_select_fusion = f32[40,8,23,256]{3,1,2,0:T(8,128)S(1)} fusion(pred[8,23]{0,1:T(8,128)(4,1)S(1)} %copy-done.9, bf16[3,3,256,256]{3,2,1,0:T(8,128)(2,1)S(1)} %copy-done, bf16[42,1,7,2,256]{4,2,3,0,1:T(8,128)(2,1)S(1)} %slice.36, bf16[42,1,8,23,256]{4,2,3,0,1:T(8,128)(2,1)S(1)} %copy.49), kind=kOutput, calls=%fused_computation.44 | convolution fusion | flops 8696995840 | bytes 12974264 | tf_op jit(solution)/shard_map/conv_general_dilated | solution.py:24
  38.8 2.6 %copy.50 = f32[40,8,23,256]{3,0,2,1:T(8,128)S(1)} copy(f32[40,8,23,256]{3,1,2,0:T(8,128)S(1)} %broadcast_select_fusion) | data formatting | bytes 15073280 | tf_op jit(solution)/shard_map/conv_general_dilated | solution.py:24
  41.4 4.2 %fusion.23 = f32[40,180,256]{2,0,1:T(8,128)} fusion(f32[40,1,184,256]{3,0,2,1:T(8,128)S(1)} %bitcast.42), kind=kLoop, calls=%fused_computation.33 | loop fusion | flops 14745600 | bytes 14745600 | tf_op jit(solution)/shard_map/mul | solution.py:57
  45.5 8.4 %reduce_window.7 = f32[20,90,256]{2,0,1:T(8,128)S(1)} reduce-window(f32[40,180,256]{2,0,1:T(8,128)} %fusion.23, f32[]{:T(128)} %constant.14.clone.1), window={size=2x2x1 stride=2x2x1}, to_apply=%region_0.0 | reduce-window | flops 1382400 | bytes 9216004 | tf_op jit(solution)/shard_map/reduce_window | solution.py:36
  53.9 0.2 multiply_convert_fusion
  54.1 0.2 copy.51
  54.4 0.2 convert_element_type.27
  54.6 0.4 convolution_convert_fusion
  55.0 0.1 reshape.13
  55.1 1.0 copy.52
  56.1 0.0 all-gather.2.cloned.1.call-update
  56.2 0.1 dynamic_slice.3
  56.3 1.2 convolution_add_fusion
  57.5 0.3 fusion.36
  57.8 33.8 %all-gather.2.cloned.1.call-done = bf16[20,720,128]{2,0,1:T(8,128)(2,1)} async-done(((bf16[20,90,128]{2,0,1:T(8,128)(2,1)}), bf16[20,720,128]{2,0,1:T(8,128)(2,1)}) %all-gather.2.cloned.1.call-update) | async-done | bytes 3686416 | tf_op jit(solution)/shard_map/all_gather | solution.py:63
  91.5 5.8 %copy_convert_fusion = f32[20,720,128]{2,1,0:T(8,128)} fusion(bf16[20,720,128]{2,0,1:T(8,128)(2,1)} %all-gather.2.cloned.1.call-done), kind=kLoop, calls=%fused_computation.45 | loop fusion | flops 1843200 | bytes 11059200 | tf_op jit(solution)/shard_map/convert_element_type | solution.py:47
  97.3 7.6 %add_convert_fusion = bf16[2,20,720,128]{3,2,1,0:T(8,128)(2,1)} fusion(f32[2,128]{1,0:T(2,128)S(1)} %fusion.36, f32[2,128]{1,0:T(2,128)S(1)} %convolution_add_fusion, f32[20,720,128]{2,1,0:T(8,128)} %copy_convert_fusion), kind=kLoop, calls=%fused_computation.13 | loop fusion | flops 11059200 | bytes 14747648 | tf_op jit(solution)/shard_map/convert_element_type | solution.py:48
  105.0 1.1 fusion.42
  106.1 3.1 %collective-permute-start.4 = (bf16[2,1,720,128]{3,2,1,0:T(8,128)(2,1)S(1)}, bf16[2,1,720,128]{3,2,1,0:T(8,128)(2,1)S(1)}, u32[]{:S(2)}, u32[]{:S(2)}) collective-permute-start(bf16[2,1,720,128]{3,2,1,0:T(8,128)(2,1)S(1)} %get-tuple-element.5), channel_id=1, source_target_pairs={{0,8},{8,16},{16,24},{24,32},{32,40},{40,48},{48,56},{56,64},{64,7... | collective-permute-start | bytes 1105928 | tf_op jit(solution)/shard_map/ppermute | solution.py:16
  109.3 2.7 %collective-permute-start.5 = (bf16[2,1,720,128]{3,2,1,0:T(8,128)(2,1)S(1)}, bf16[2,1,720,128]{3,2,1,0:T(8,128)(2,1)S(1)}, u32[]{:S(2)}, u32[]{:S(2)}) collective-permute-start(bf16[2,1,720,128]{3,2,1,0:T(8,128)(2,1)S(1)} %get-tuple-element.6), channel_id=1, source_target_pairs={{8,0},{16,8},{24,16},{32,24},{40,32},{48,40},{56,48},{64,56},{72,6... | collective-permute-start | bytes 1105928 | tf_op jit(solution)/shard_map/ppermute | solution.py:17
  112.0 6.8 %collective-permute-done.4 = bf16[2,1,720,128]{3,2,1,0:T(8,128)(2,1)S(1)} collective-permute-done((bf16[2,1,720,128]{3,2,1,0:T(8,128)(2,1)S(1)}, bf16[2,1,720,128]{3,2,1,0:T(8,128)(2,1)S(1)}, u32[]{:S(2)}, u32[]{:S(2)}) %collective-permute-start.4) | collective-permute-done | bytes 368672 | tf_op jit(solution)/shard_map/ppermute | solution.py:16
  118.8 5.0 %collective-permute-done.5 = bf16[2,1,720,128]{3,2,1,0:T(8,128)(2,1)S(1)} collective-permute-done((bf16[2,1,720,128]{3,2,1,0:T(8,128)(2,1)S(1)}, bf16[2,1,720,128]{3,2,1,0:T(8,128)(2,1)S(1)}, u32[]{:S(2)}, u32[]{:S(2)}) %collective-permute-start.5) | collective-permute-done | bytes 368672 | tf_op jit(solution)/shard_map/ppermute | solution.py:17
  123.7 13.0 %fusion.15 = bf16[22,2,722,128]{3,2,0,1:T(8,128)(2,1)} fusion(bf16[2,1,720,128]{3,2,1,0:T(8,128)(2,1)S(1)} %collective-permute-done.5, bf16[2,20,720,128]{3,2,1,0:T(8,128)(2,1)} %add_convert_fusion, bf16[2,1,720,128]{3,2,1,0:T(8,128)(2,1)S(1)} %collective-permute-done.4), kind=kLoop, calls=%fused_computation.22 | loop fusion | flops 73193472 | bytes 16242688 | tf_op jit(solution)/shard_map/concatenate | solution.py:43
  136.8 7.0 %pad.2 = bf16[22,2,728,128]{3,2,0,1:T(8,128)(2,1)} pad(bf16[22,2,722,128]{3,2,0,1:T(8,128)(2,1)} %fusion.15, bf16[]{:T(256)} %constant.6), padding=0_0x0_0x0_6x0_0 | pad | bytes 16332802 | tf_op jit(solution)/shard_map/concatenate | solution.py:43
  143.8 12.6 %reshape.39 = bf16[22,2,8,91,128]{4,3,2,0,1:T(8,128)(2,1)} reshape(bf16[22,2,728,128]{3,2,0,1:T(8,128)(2,1)} %pad.2) | data formatting | bytes 16400384 | tf_op jit(solution)/shard_map/conv_general_dilated | solution.py:24
  156.3 1.2 slice.40
  157.5 0.1 copy.77
  157.7 4.6 %fusion.10 = bf16[22,2,8,93,128]{4,3,2,1,0:T(8,128)(2,1)S(1)} fusion(bf16[22,2,7,2,128]{4,3,2,1,0:T(2,128)(2,1)S(1)} %copy.77, bf16[22,2,8,91,128]{4,3,2,0,1:T(8,128)(2,1)} %reshape.39), kind=kLoop, calls=%fused_computation.15 | loop fusion | flops 25141248 | bytes 16738304 | tf_op jit(solution)/shard_map/conv_general_dilated | solution.py:24
  162.3 21.3 %fusion.8 = bf16[20,16,91,128]{3,1,2,0:T(8,128)(2,1)S(1)} fusion(bf16[3,3,128,128]{3,2,1,0:T(8,128)(2,1)S(1)} %copy-done.6, bf16[22,2,8,93,128]{4,3,2,1,0:T(8,128)(2,1)S(1)} %fusion.10, pred[16,91]{0,1:T(8,128)(4,1)S(1)} %copy-done.8), kind=kOutput, calls=%fused_computation.10 | convolution fusion | flops 8625111040 | bytes 16131504 | tf_op jit(solution)/shard_map/conv_general_dilated | solution.py:24
  183.6 5.1 %copy.56 = bf16[20,16,91,128]{3,2,1,0:T(8,128)(2,1)} copy(bf16[20,16,91,128]{3,1,2,0:T(8,128)(2,1)S(1)} %fusion.8) | data formatting | bytes 14909440 | tf_op jit(solution)/shard_map/convert_element_type | solution.py:79
  188.7 11.6 %reshape.27 = bf16[20,2,728,128]{3,2,1,0:T(8,128)(2,1)} reshape(bf16[20,16,91,128]{3,2,1,0:T(8,128)(2,1)} %copy.56) | data formatting | bytes 14909440 | tf_op jit(solution)/shard_map/convert_element_type | solution.py:79
  200.3 12.3 %fusion.9 = bf16[2,20,720,128]{3,2,1,0:T(8,128)(2,1)} fusion(bf16[2,20,720,128]{3,2,1,0:T(8,128)(2,1)} %add_convert_fusion, bf16[720,720]{1,0:T(8,128)(2,1)S(1)} %copy-done.5, bf16[20,2,728,128]{3,2,1,0:T(8,128)(2,1)} %reshape.27), kind=kOutput, calls=%fused_computation.12 | convolution fusion | flops 5319475200 | bytes 23155200 | tf_op jit(solution)/shard_map/ij,bajc->baic/dot_general | solution.py:80
  (23 shorter events, 0.1 us)
Async XLA Ops:
  6.5 22.7 %copy-start = (bf16[3,3,256,256]{3,2,1,0:T(8,128)(2,1)S(1)}, bf16[3,3,256,256]{3,2,1,0:T(8,128)(2,1)}, u32[]{:S(2)}) copy-start(bf16[3,3,256,256]{3,2,1,0:T(8,128)(2,1)} %param.9) | copy-start | bytes 3538948
  6.5 85.0 %all-gather.2.cloned.1.call-start = ((), (), s32[]{:S(2)}) async-start(), calls=%async_computation | async-start | bytes 4976640 | tf_op jit(solution)/shard_map/all_gather | solution.py:63
  6.5 17.5 %copy-start.2 = (bf16[40,180,256]{2,0,1:T(8,128)(2,1)S(1)}, bf16[40,180,256]{2,0,1:T(8,128)(2,1)}, u32[]{:S(2)}) copy-start(bf16[40,180,256]{2,0,1:T(8,128)(2,1)} %param.8) | copy-start | bytes 11059204
  8.4 8.7 %collective-permute-start.1 = (bf16[1,180,256]{2,1,0:T(8,128)(2,1)S(1)}, bf16[1,180,256]{2,1,0:T(8,128)(2,1)S(1)}, u32[]{:S(2)}, u32[]{:S(2)}) collective-permute-start(bf16[1,180,256]{2,1,0:T(8,128)(2,1)S(1)} %copy.64), channel_id=1, source_target_pairs={{8,0},{16,8},{24,16},{32,24},{40,32},{48,40},{56,48},{64,56},{72,6... | collective-permute-start | bytes 276488 | tf_op jit(solution)/shard_map/ppermute | solution.py:17
  10.8 7.8 %collective-permute-start = (bf16[1,180,256]{2,1,0:T(8,128)(2,1)S(1)}, bf16[1,180,256]{2,1,0:T(8,128)(2,1)S(1)}, u32[]{:S(2)}, u32[]{:S(2)}) collective-permute-start(bf16[1,180,256]{2,1,0:T(8,128)(2,1)S(1)} %copy.63), channel_id=1, source_target_pairs={{0,8},{8,16},{16,24},{24,32},{32,40},{40,48},{48,56},{56,64},{64,7... | collective-permute-start | bytes 276488 | tf_op jit(solution)/shard_map/ppermute | solution.py:16
  19.5 4.5 %collective-permute-start.2 = (bf16[42,1,256]{2,0,1:T(8,128)(2,1)S(1)}, bf16[42,1,256]{2,0,1:T(8,128)(2,1)S(1)}, u32[]{:S(2)}, u32[]{:S(2)}) collective-permute-start(bf16[42,1,256]{2,0,1:T(8,128)(2,1)S(1)} %get-tuple-element.7), channel_id=1, source_target_pairs={{0,1},{1,2},{2,3},{3,4},{4,5},{5,6},{6,7},{7,0},{8,9},{9,10},{10,1... | collective-permute-start | bytes 64520 | tf_op jit(solution)/shard_map/ppermute | solution.py:16
  19.6 4.5 %collective-permute-start.3 = (bf16[42,1,256]{2,0,1:T(8,128)(2,1)S(1)}, bf16[42,1,256]{2,0,1:T(8,128)(2,1)S(1)}, u32[]{:S(2)}, u32[]{:S(2)}) collective-permute-start(bf16[42,1,256]{2,0,1:T(8,128)(2,1)S(1)} %get-tuple-element.8), channel_id=1, source_target_pairs={{1,0},{2,1},{3,2},{4,3},{5,4},{6,5},{7,6},{0,7},{9,8},{10,9},{11,1... | collective-permute-start | bytes 64520 | tf_op jit(solution)/shard_map/ppermute | solution.py:17
  27.2 2.0 copy-start.9
  45.5 9.1 %copy-start.4 = (bf16[256,128]{1,0:T(8,128)(2,1)S(1)}, bf16[256,128]{1,0:T(8,128)(2,1)}, u32[]{:S(2)}) copy-start(bf16[256,128]{1,0:T(8,128)(2,1)} %param.10) | copy-start | bytes 196612
  45.5 10.7 %copy-start.7 = (s32[16]{0:T(128)S(1)}, s32[16]{0:T(128)}, u32[]{:S(2)}) copy-start(s32[16]{0:T(128)} %param.13) | copy-start | bytes 196
  54.1 3.4 %copy-start.3 = (f32[720,128]{1,0:T(8,128)S(1)}, f32[720,128]{1,0:T(8,128)}, u32[]{:S(2)}) copy-start(f32[720,128]{1,0:T(8,128)} %param.12) | copy-start | bytes 1105924
  106.1 12.6 %collective-permute-start.4 = (bf16[2,1,720,128]{3,2,1,0:T(8,128)(2,1)S(1)}, bf16[2,1,720,128]{3,2,1,0:T(8,128)(2,1)S(1)}, u32[]{:S(2)}, u32[]{:S(2)}) collective-permute-start(bf16[2,1,720,128]{3,2,1,0:T(8,128)(2,1)S(1)} %get-tuple-element.5), channel_id=1, source_target_pairs={{0,8},{8,16},{16,24},{24,32},{32,40},{40,48},{48,56},{56,64},{64,7... | collective-permute-start | bytes 1105928 | tf_op jit(solution)/shard_map/ppermute | solution.py:16
  109.3 14.5 %collective-permute-start.5 = (bf16[2,1,720,128]{3,2,1,0:T(8,128)(2,1)S(1)}, bf16[2,1,720,128]{3,2,1,0:T(8,128)(2,1)S(1)}, u32[]{:S(2)}, u32[]{:S(2)}) collective-permute-start(bf16[2,1,720,128]{3,2,1,0:T(8,128)(2,1)S(1)} %get-tuple-element.6), channel_id=1, source_target_pairs={{8,0},{16,8},{24,16},{32,24},{40,32},{48,40},{56,48},{64,56},{72,6... | collective-permute-start | bytes 1105928 | tf_op jit(solution)/shard_map/ppermute | solution.py:17
  157.7 4.6 %copy-start.6 = (bf16[3,3,128,128]{3,2,1,0:T(8,128)(2,1)S(1)}, bf16[3,3,128,128]{3,2,1,0:T(8,128)(2,1)}, u32[]{:S(2)}) copy-start(bf16[3,3,128,128]{3,2,1,0:T(8,128)(2,1)} %param.14) | copy-start | bytes 884740
  157.7 4.6 %copy-start.8 = (pred[16,91]{0,1:T(8,128)(4,1)S(1)}, pred[16,91]{0,1:T(8,128)(4,1)}, u32[]{:S(2)}) copy-start(pred[16,91]{0,1:T(8,128)(4,1)} %constant.37) | copy-start | bytes 4372
  188.7 11.6 %copy-start.5 = (bf16[720,720]{1,0:T(8,128)(2,1)S(1)}, bf16[720,720]{1,0:T(8,128)(2,1)}, u32[]{:S(2)}) copy-start(bf16[720,720]{1,0:T(8,128)(2,1)} %param.15) | copy-start | bytes 3110404
  200.3 12.3 %copy-start.1 = (bf16[3,3,256,256]{3,2,1,0:T(8,128)(2,1)S(1)}, bf16[3,3,256,256]{3,2,1,0:T(8,128)(2,1)}, u32[]{:S(2)}) copy-start(bf16[3,3,256,256]{3,2,1,0:T(8,128)(2,1)} %param.9) | copy-start | bytes 3538948
Sparse Core Ops, SparseCore 0:
  56.3 35.2 all-gather.1
where the time goes:
time: 223 us; the launch traced here: 220 us
  waiting for transfers between devices  49.1 us (22%)
  other arithmetic  47.8 us (21%)
  local copies, waits for them, and re-layouts  47 us (21%)
  matrix products  45 us (20%)
  starting transfers between devices  16.9 us (8%)
  between operations  13.9 us (6%)
    all_gather x1, waiting for transfers between devices, shards(): lax.all_gather(flat.astype(jnp.bfloat16).reshape(pooled.shape[0], pooled....  33.8 us
    conv_general_dilated x2, matrix products, conv_three(): lax.conv_general_dilated(batched, weight, (1, 1), 'VALID', dimension_numb...  30.8 us
    conv_general_dilated x5, local copies, waits for them, and re-layouts, conv_three(): lax.conv_general_dilated(batched, weight, (1, 1), 'VALID', dimension_numb...  17.9 us
    convert_element_type x2, local copies, waits for them, and re-layouts, shards(): hidden = jax.nn.gelu(conv_three(padded_head, w_head)).astype(jnp.bfloat16)  16.7 us
    concatenate x1, other arithmetic, wrap_columns(): jnp.concatenate([field[..., -1:, :], field, field[..., :1, :]], axis=-2)  13 us
    dot_general x1, matrix products, shards(): jnp.einsum('ij,bajc->baic', zonal_mix, hidden, preferred_element_type=jnp...  12.3 us
    ppermute x3, waiting for transfers between devices, extended(): before = lax.ppermute(last, axis, up)  9.7 us
    ppermute x3, starting transfers between devices, extended(): before = lax.ppermute(last, axis, up)  8.78 us
  transfers between devices with their start and end apart: 7, of which 6 were waited for; matrix products, arithmetic and copies ran while one was open for 1% of the time, Pallas kernels for 0%

commit v1 on v0

--- a/solution.py
+++ b/solution.py
@@ -60,11 +60,17 @@
     lon_group = lax.axis_index("lon")
     my_rows = lax.dynamic_slice_in_dim(lead_ids, lon_group * LEAD_DEV, LEAD_DEV)
     flat = jnp.dot(pooled.reshape(-1, channels), w_proj, preferred_element_type=jnp.float32)
-    band_proj = lax.all_gather(
-        flat.astype(jnp.bfloat16).reshape(pooled.shape[0], pooled.shape[1], head_width),
-        "lon",
+    band_proj = jnp.concatenate(
+        lax.all_to_all(
+            jnp.stack(
+                [flat.astype(jnp.bfloat16).reshape(pooled.shape[0], pooled.shape[1], head_width)]
+                * lax.axis_size("lon")
+            ),
+            "lon",
+            0,
+            0,
+        ),
         axis=1,
-        tiled=True,
     )
     onehot = (my_rows[:, None] == jnp.arange(film_scale.shape[0], dtype=jnp.int32)[None, :]).astype(
         jnp.float32

time: 223 us -> 240 us (1.076)
  local copies, waits for them, and re-layouts: 47 us -> 61.1 us
  between operations: 13.9 us -> 0.58 us
  waiting for transfers between devices: 49.1 us -> 61.7 us
  starting transfers between devices: 16.9 us -> 23.9 us
  other arithmetic: 47.8 us -> 45.2 us
    all_to_all x0 -> x1, waiting for transfers between devices: none -> 46.2 us  [shards(): lax.all_to_all(jnp.stack([flat.astype(jnp.bfloat16).reshape(pooled.shape[...]
    all_gather x1 -> x0, waiting for transfers between devices: 33.8 us -> none  [shards(): lax.all_gather(flat.astype(jnp.bfloat16).reshape(pooled.shape[0], pooled....]
    convert_element_type x0 -> x2, local copies, waits for them, and re-layouts: none -> 12.5 us  [modulate(): widened = projected.astype(jnp.float32)[None]]
    all_to_all x0 -> x1, starting transfers between devices: none -> 4.52 us  [shards(): lax.all_to_all(jnp.stack([flat.astype(jnp.bfloat16).reshape(pooled.shape[...]
    ppermute x3, starting transfers between devices: 8.78 us -> 12.1 us  [extended(): before = lax.ppermute(last, axis, up)]
    another operation x0 -> x2, local copies, waits for them, and re-layouts: none -> 2.71 us  [shards(): jnp.stack([flat.astype(jnp.bfloat16).reshape(pooled.shape[0], pooled.shap...]
    convert_element_type x1, other arithmetic: 5.79 us -> 3.19 us  [modulate(): widened = projected.astype(jnp.float32)[None]]
  transfers between devices with their start and end apart: 7 -> 7, of which waited for: 6 -> 6; matrix products, arithmetic and copies ran while one was open for 1% -> 0% of each run, Pallas kernels for 0% -> 0%
where the time goes in v1:
time: 240 us; the launch traced here: 236 us
  waiting for transfers between devices  61.7 us (26%)
  local copies, waits for them, and re-layouts  61.1 us (25%)
  other arithmetic  45.2 us (19%)
  matrix products  44 us (18%)
  starting transfers between devices  23.9 us (10%)
    all_to_all x1, waiting for transfers between devices, shards(): lax.all_to_all(jnp.stack([flat.astype(jnp.bfloat16).reshape(pooled.shape[...  46.2 us
    conv_general_dilated x2, matrix products, conv_three(): lax.conv_general_dilated(batched, weight, (1, 1), 'VALID', dimension_numb...  30.8 us
    conv_general_dilated x5, local copies, waits for them, and re-layouts, conv_three(): lax.conv_general_dilated(batched, weight, (1, 1), 'VALID', dimension_numb...  17.9 us
    convert_element_type x2, local copies, waits for them, and re-layouts, shards(): hidden = jax.nn.gelu(conv_three(padded_head, w_head)).astype(jnp.bfloat16)  16.7 us
    concatenate x1, other arithmetic, wrap_columns(): jnp.concatenate([field[..., -1:, :], field, field[..., :1, :]], axis=-2)  13 us
    convert_element_type x2, local copies, waits for them, and re-layouts, modulate(): widened = projected.astype(jnp.float32)[None]  12.5 us
    dot_general x1, matrix products, shards(): jnp.einsum('ij,bajc->baic', zonal_mix, hidden, preferred_element_type=jnp...  12.3 us
    ppermute x3, starting transfers between devices, extended(): before = lax.ppermute(last, axis, up)  12.1 us
  transfers between devices with their start and end apart: 7, of which 6 were waited for; matrix products, arithmetic and copies ran while one was open for 0% of the time, Pallas kernels for 0%

profile of v1, /device:TPU:96, one launch (start us, length us, event | category | flops | bytes accessed | tf_op | source)
XLA Modules:
  0.0 236.5 jit_solution(2399598342748320848)
XLA Ops:
  0.0 1.8 fusion.43
  1.8 2.4 %collective-permute-start.1 = (bf16[1,180,256]{2,1,0:T(8,128)(2,1)S(1)}, bf16[1,180,256]{2,1,0:T(8,128)(2,1)S(1)}, u32[]{:S(2)}, u32[]{:S(2)}) collective-permute-start(bf16[1,180,256]{2,1,0:T(8,128)(2,1)S(1)} %copy.48), channel_id=1, source_target_pairs={{8,0},{16,8},{24,16},{32,24},{40,32},{48,40},{56,48},{64,56},{72,6... | collective-permute-start | bytes 276488 | tf_op jit(solution)/shard_map/ppermute | solution.py:17
  4.3 5.6 %collective-permute-start = (bf16[1,180,256]{2,1,0:T(8,128)(2,1)S(1)}, bf16[1,180,256]{2,1,0:T(8,128)(2,1)S(1)}, u32[]{:S(2)}, u32[]{:S(2)}) collective-permute-start(bf16[1,180,256]{2,1,0:T(8,128)(2,1)S(1)} %copy.47), channel_id=1, source_target_pairs={{0,8},{8,16},{16,24},{24,32},{32,40},{40,48},{48,56},{56,64},{64,7... | collective-permute-start | bytes 276488 | tf_op jit(solution)/shard_map/ppermute | solution.py:16
  9.9 0.6 collective-permute-done.1
  10.5 0.1 copy.31
  10.7 1.4 collective-permute-done
  12.1 0.1 copy.30
  12.2 0.8 pad_maximum_fusion.6
  13.0 2.9 %collective-permute-start.3 = (bf16[42,1,256]{2,0,1:T(8,128)(2,1)S(1)}, bf16[42,1,256]{2,0,1:T(8,128)(2,1)S(1)}, u32[]{:S(2)}, u32[]{:S(2)}) collective-permute-start(bf16[42,1,256]{2,0,1:T(8,128)(2,1)S(1)} %get-tuple-element.8), channel_id=1, source_target_pairs={{1,0},{2,1},{3,2},{4,3},{5,4},{6,5},{7,6},{0,7},{9,8},{10,9},{11,1... | collective-permute-start | bytes 64520 | tf_op jit(solution)/shard_map/ppermute | solution.py:17
  16.0 1.5 collective-permute-done.2
  17.5 3.2 %maximum_bitcast_fusion = bf16[42,1,182,256]{3,0,2,1:T(8,128)(2,1)S(1)} fusion(bf16[42,1,256]{2,0,1:T(8,128)(2,1)S(1)} %collective-permute-done.3, bf16[1,180,256]{2,0,1:T(2,128)(2,1)S(1)} %copy.31, bf16[40,180,256]{2,0,1:T(8,128)(2,1)S(1)} %copy-done.2, bf16[1,180,256]{2,0,1:T(2,128)(2,1)S(1)} %copy.30, bf16[42,1,256]{2,0,1:T(8,128)(2,1)S(1)} %collective-permute-done.2), kind=kLoop, calls=%fused_computation.38 | loop fusion | flops 19568640 | bytes 7827456 | tf_op jit(solution)/shard_map/broadcast_in_dim | solution.py:23
  20.7 0.4 pad
  21.1 1.5 copy.34
  22.6 0.1 slice.36
  22.7 9.5 %broadcast_select_fusion = f32[40,8,23,256]{3,1,2,0:T(8,128)S(1)} fusion(pred[8,23]{0,1:T(8,128)(4,1)S(1)} %copy-done.10, bf16[3,3,256,256]{3,2,1,0:T(8,128)(2,1)S(1)} %copy-done, bf16[42,1,7,2,256]{4,2,3,0,1:T(8,128)(2,1)S(1)} %slice.36, bf16[42,1,8,23,256]{4,2,3,0,1:T(8,128)(2,1)S(1)} %copy.34), kind=kOutput, calls=%fused_computation.45 | convolution fusion | flops 8696995840 | bytes 12974264 | tf_op jit(solution)/shard_map/conv_general_dilated | solution.py:24
  32.2 2.6 %copy.35 = f32[40,8,23,256]{3,0,2,1:T(8,128)S(1)} copy(f32[40,8,23,256]{3,1,2,0:T(8,128)S(1)} %broadcast_select_fusion) | data formatting | bytes 15073280 | tf_op jit(solution)/shard_map/conv_general_dilated | solution.py:24
  34.8 4.2 %fusion.23 = f32[40,180,256]{2,0,1:T(8,128)} fusion(f32[40,1,184,256]{3,0,2,1:T(8,128)S(1)} %bitcast.44), kind=kLoop, calls=%fused_computation.34 | loop fusion | flops 14745600 | bytes 14745600 | tf_op jit(solution)/shard_map/mul | solution.py:57
  39.0 8.4 %reduce_window.7 = f32[20,90,256]{2,0,1:T(8,128)S(1)} reduce-window(f32[40,180,256]{2,0,1:T(8,128)} %fusion.23, f32[]{:T(128)} %constant.14.clone.1), window={size=2x2x1 stride=2x2x1}, to_apply=%region_0.0 | reduce-window | flops 1382400 | bytes 9216004 | tf_op jit(solution)/shard_map/reduce_window | solution.py:36
  47.4 0.2 multiply_convert_fusion
  47.6 0.2 copy.36
  47.8 0.2 convert_element_type.37
  48.1 0.4 convolution_convert_fusion
  48.5 0.1 stack_reshape.2
  48.6 2.6 %stack.3 = bf16[8,20,90,128]{3,2,1,0:T(8,128)(2,1)} broadcast(bf16[20,90,128]{2,1,0:T(8,128)(2,1)S(1)} %stack_reshape.2), dimensions={1,2,3} | broadcast | bytes 4147200 | tf_op jit(solution)/shard_map/stack | solution.py:65
  51.2 4.5 %all-to-all-start = ((bf16[8,20,90,128]{3,2,1,0:T(8,128)(2,1)}), bf16[8,20,90,128]{3,2,1,0:T(8,128)(2,1)}, u32[]{:S(2)}, u32[]{:S(2)}) async-start(bf16[8,20,90,128]{3,2,1,0:T(8,128)(2,1)} %stack.3), calls=%async_computation | async-start | bytes 7864320 | tf_op jit(solution)/shard_map/all_to_all | solution.py:64
  55.8 0.1 dynamic_slice.3
  55.8 0.3 convolution_add_fusion
  56.1 0.3 fusion.36
  56.4 46.2 %all-to-all-done = bf16[8,20,90,128]{3,2,1,0:T(8,128)(2,1)} async-done(((bf16[8,20,90,128]{3,2,1,0:T(8,128)(2,1)}), bf16[8,20,90,128]{3,2,1,0:T(8,128)(2,1)}, u32[]{:S(2)}, u32[]{:S(2)}) %all-to-all-start) | async-done | bytes 3686432 | tf_op jit(solution)/shard_map/all_to_all | solution.py:64
  102.6 3.2 %convert_bitcast_fusion = f32[20,8,90,128]{3,2,0,1:T(8,128)S(1)} fusion(bf16[8,20,90,128]{3,2,1,0:T(8,128)(2,1)} %all-to-all-done), kind=kLoop, calls=%fused_computation.27 | loop fusion | flops 1843200 | bytes 11059200 | tf_op jit(solution)/shard_map/convert_element_type | solution.py:47
  105.8 4.0 %copy.37 = f32[20,8,90,128]{3,2,1,0:T(8,128)} copy(f32[20,8,90,128]{3,2,0,1:T(8,128)S(1)} %convert_bitcast_fusion) | data formatting | bytes 14745600 | tf_op jit(solution)/shard_map/convert_element_type | solution.py:47
  109.8 8.5 %reshape.34 = f32[20,720,128]{2,1,0:T(8,128)} reshape(f32[20,8,90,128]{3,2,1,0:T(8,128)} %copy.37) | data formatting | bytes 14745600 | tf_op jit(solution)/shard_map/convert_element_type | solution.py:47
  118.3 7.6 %add_convert_fusion = bf16[2,20,720,128]{3,2,1,0:T(8,128)(2,1)} fusion(f32[2,128]{1,0:T(2,128)S(1)} %fusion.36, f32[2,128]{1,0:T(2,128)S(1)} %convolution_add_fusion, f32[20,720,128]{2,1,0:T(8,128)} %reshape.34), kind=kLoop, calls=%fused_computation.13 | loop fusion | flops 11059200 | bytes 14747648 | tf_op jit(solution)/shard_map/convert_element_type | solution.py:48
  125.9 1.1 fusion.42
  127.1 6.4 %collective-permute-start.4 = (bf16[2,1,720,128]{3,2,1,0:T(8,128)(2,1)S(1)}, bf16[2,1,720,128]{3,2,1,0:T(8,128)(2,1)S(1)}, u32[]{:S(2)}, u32[]{:S(2)}) collective-permute-start(bf16[2,1,720,128]{3,2,1,0:T(8,128)(2,1)S(1)} %get-tuple-element.5), channel_id=1, source_target_pairs={{0,8},{8,16},{16,24},{24,32},{32,40},{40,48},{48,56},{56,64},{64,7... | collective-permute-start | bytes 1105928 | tf_op jit(solution)/shard_map/ppermute | solution.py:16
  133.5 1.9 collective-permute-start.5
  135.4 5.7 %collective-permute-done.4 = bf16[2,1,720,128]{3,2,1,0:T(8,128)(2,1)S(1)} collective-permute-done((bf16[2,1,720,128]{3,2,1,0:T(8,128)(2,1)S(1)}, bf16[2,1,720,128]{3,2,1,0:T(8,128)(2,1)S(1)}, u32[]{:S(2)}, u32[]{:S(2)}) %collective-permute-start.4) | collective-permute-done | bytes 368672 | tf_op jit(solution)/shard_map/ppermute | solution.py:16
  141.1 6.2 %collective-permute-done.5 = bf16[2,1,720,128]{3,2,1,0:T(8,128)(2,1)S(1)} collective-permute-done((bf16[2,1,720,128]{3,2,1,0:T(8,128)(2,1)S(1)}, bf16[2,1,720,128]{3,2,1,0:T(8,128)(2,1)S(1)}, u32[]{:S(2)}, u32[]{:S(2)}) %collective-permute-start.5) | collective-permute-done | bytes 368672 | tf_op jit(solution)/shard_map/ppermute | solution.py:17
  147.4 13.0 %fusion.15 = bf16[22,2,722,128]{3,2,0,1:T(8,128)(2,1)} fusion(bf16[2,1,720,128]{3,2,1,0:T(8,128)(2,1)S(1)} %collective-permute-done.5, bf16[2,20,720,128]{3,2,1,0:T(8,128)(2,1)} %add_convert_fusion, bf16[2,1,720,128]{3,2,1,0:T(8,128)(2,1)S(1)} %collective-permute-done.4), kind=kLoop, calls=%fused_computation.22 | loop fusion | flops 73193472 | bytes 16242688 | tf_op jit(solution)/shard_map/concatenate | solution.py:43
  160.4 7.0 %pad.2 = bf16[22,2,728,128]{3,2,0,1:T(8,128)(2,1)} pad(bf16[22,2,722,128]{3,2,0,1:T(8,128)(2,1)} %fusion.15, bf16[]{:T(256)} %constant.6), padding=0_0x0_0x0_6x0_0 | pad | bytes 16332802 | tf_op jit(solution)/shard_map/concatenate | solution.py:43
  167.4 12.6 %reshape.46 = bf16[22,2,8,91,128]{4,3,2,0,1:T(8,128)(2,1)} reshape(bf16[22,2,728,128]{3,2,0,1:T(8,128)(2,1)} %pad.2) | data formatting | bytes 16400384 | tf_op jit(solution)/shard_map/conv_general_dilated | solution.py:24
  180.0 1.2 slice.40
  181.2 0.1 copy.60
  181.3 4.6 %fusion.10 = bf16[22,2,8,93,128]{4,3,2,1,0:T(8,128)(2,1)S(1)} fusion(bf16[22,2,7,2,128]{4,3,2,1,0:T(2,128)(2,1)S(1)} %copy.60, bf16[22,2,8,91,128]{4,3,2,0,1:T(8,128)(2,1)} %reshape.46), kind=kLoop, calls=%fused_computation.15 | loop fusion | flops 25141248 | bytes 16738304 | tf_op jit(solution)/shard_map/conv_general_dilated | solution.py:24
  186.0 21.3 %fusion.8 = bf16[20,16,91,128]{3,1,2,0:T(8,128)(2,1)S(1)} fusion(bf16[3,3,128,128]{3,2,1,0:T(8,128)(2,1)S(1)} %copy-done.7, bf16[22,2,8,93,128]{4,3,2,1,0:T(8,128)(2,1)S(1)} %fusion.10, pred[16,91]{0,1:T(8,128)(4,1)S(1)} %copy-done.9), kind=kOutput, calls=%fused_computation.10 | convolution fusion | flops 8625111040 | bytes 16131504 | tf_op jit(solution)/shard_map/conv_general_dilated | solution.py:24
  207.3 5.1 %copy.40 = bf16[20,16,91,128]{3,2,1,0:T(8,128)(2,1)} copy(bf16[20,16,91,128]{3,1,2,0:T(8,128)(2,1)S(1)} %fusion.8) | data formatting | bytes 14909440 | tf_op jit(solution)/shard_map/convert_element_type | solution.py:85
  212.4 11.6 %reshape.33 = bf16[20,2,728,128]{3,2,1,0:T(8,128)(2,1)} reshape(bf16[20,16,91,128]{3,2,1,0:T(8,128)(2,1)} %copy.40) | data formatting | bytes 14909440 | tf_op jit(solution)/shard_map/convert_element_type | solution.py:85
  223.9 12.3 %fusion.9 = bf16[2,20,720,128]{3,2,1,0:T(8,128)(2,1)} fusion(bf16[2,20,720,128]{3,2,1,0:T(8,128)(2,1)} %add_convert_fusion, bf16[720,720]{1,0:T(8,128)(2,1)S(1)} %copy-done.6, bf16[20,2,728,128]{3,2,1,0:T(8,128)(2,1)} %reshape.33), kind=kOutput, calls=%fused_computation.12 | convolution fusion | flops 5319475200 | bytes 23155200 | tf_op jit(solution)/shard_map/ij,bajc->baic/dot_general | solution.py:86
  (26 shorter events, 0.1 us)
Async XLA Ops:
  0.0 22.7 %copy-start = (bf16[3,3,256,256]{3,2,1,0:T(8,128)(2,1)S(1)}, bf16[3,3,256,256]{3,2,1,0:T(8,128)(2,1)}, u32[]{:S(2)}) copy-start(bf16[3,3,256,256]{3,2,1,0:T(8,128)(2,1)} %param.9) | copy-start | bytes 3538948
  0.0 17.5 %copy-start.2 = (bf16[40,180,256]{2,0,1:T(8,128)(2,1)S(1)}, bf16[40,180,256]{2,0,1:T(8,128)(2,1)}, u32[]{:S(2)}) copy-start(bf16[40,180,256]{2,0,1:T(8,128)(2,1)} %param.8) | copy-start | bytes 11059204
  1.8 8.7 %collective-permute-start.1 = (bf16[1,180,256]{2,1,0:T(8,128)(2,1)S(1)}, bf16[1,180,256]{2,1,0:T(8,128)(2,1)S(1)}, u32[]{:S(2)}, u32[]{:S(2)}) collective-permute-start(bf16[1,180,256]{2,1,0:T(8,128)(2,1)S(1)} %copy.48), channel_id=1, source_target_pairs={{8,0},{16,8},{24,16},{32,24},{40,32},{48,40},{56,48},{64,56},{72,6... | collective-permute-start | bytes 276488 | tf_op jit(solution)/shard_map/ppermute | solution.py:17
  4.3 7.8 %collective-permute-start = (bf16[1,180,256]{2,1,0:T(8,128)(2,1)S(1)}, bf16[1,180,256]{2,1,0:T(8,128)(2,1)S(1)}, u32[]{:S(2)}, u32[]{:S(2)}) collective-permute-start(bf16[1,180,256]{2,1,0:T(8,128)(2,1)S(1)} %copy.47), channel_id=1, source_target_pairs={{0,8},{8,16},{16,24},{24,32},{32,40},{40,48},{48,56},{56,64},{64,7... | collective-permute-start | bytes 276488 | tf_op jit(solution)/shard_map/ppermute | solution.py:16
  13.0 4.5 %collective-permute-start.2 = (bf16[42,1,256]{2,0,1:T(8,128)(2,1)S(1)}, bf16[42,1,256]{2,0,1:T(8,128)(2,1)S(1)}, u32[]{:S(2)}, u32[]{:S(2)}) collective-permute-start(bf16[42,1,256]{2,0,1:T(8,128)(2,1)S(1)} %get-tuple-element.7), channel_id=1, source_target_pairs={{0,1},{1,2},{2,3},{3,4},{4,5},{5,6},{6,7},{7,0},{8,9},{9,10},{10,1... | collective-permute-start | bytes 64520 | tf_op jit(solution)/shard_map/ppermute | solution.py:16
  13.0 4.5 %collective-permute-start.3 = (bf16[42,1,256]{2,0,1:T(8,128)(2,1)S(1)}, bf16[42,1,256]{2,0,1:T(8,128)(2,1)S(1)}, u32[]{:S(2)}, u32[]{:S(2)}) collective-permute-start(bf16[42,1,256]{2,0,1:T(8,128)(2,1)S(1)} %get-tuple-element.8), channel_id=1, source_target_pairs={{1,0},{2,1},{3,2},{4,3},{5,4},{6,5},{7,6},{0,7},{9,8},{10,9},{11,1... | collective-permute-start | bytes 64520 | tf_op jit(solution)/shard_map/ppermute | solution.py:17
  20.7 2.0 copy-start.10
  39.0 9.1 %copy-start.5 = (bf16[256,128]{1,0:T(8,128)(2,1)S(1)}, bf16[256,128]{1,0:T(8,128)(2,1)}, u32[]{:S(2)}) copy-start(bf16[256,128]{1,0:T(8,128)(2,1)} %param.10) | copy-start | bytes 196612
  47.8 8.0 %copy-start.8 = (s32[16]{0:T(128)S(1)}, s32[16]{0:T(128)}, u32[]{:S(2)}) copy-start(s32[16]{0:T(128)} %param.13) | copy-start | bytes 196
  47.8 8.0 %copy-start.3 = (f32[720,128]{1,0:T(8,128)S(1)}, f32[720,128]{1,0:T(8,128)}, u32[]{:S(2)}) copy-start(f32[720,128]{1,0:T(8,128)} %param.11) | copy-start | bytes 1105924
  47.8 8.3 %copy-start.4 = (f32[720,128]{1,0:T(8,128)S(1)}, f32[720,128]{1,0:T(8,128)}, u32[]{:S(2)}) copy-start(f32[720,128]{1,0:T(8,128)} %param.12) | copy-start | bytes 1105924
  51.2 51.4 %all-to-all-start = ((bf16[8,20,90,128]{3,2,1,0:T(8,128)(2,1)}), bf16[8,20,90,128]{3,2,1,0:T(8,128)(2,1)}, u32[]{:S(2)}, u32[]{:S(2)}) async-start(bf16[8,20,90,128]{3,2,1,0:T(8,128)(2,1)} %stack.3), calls=%async_computation | async-start | bytes 7864320 | tf_op jit(solution)/shard_map/all_to_all | solution.py:64
  127.1 14.0 %collective-permute-start.4 = (bf16[2,1,720,128]{3,2,1,0:T(8,128)(2,1)S(1)}, bf16[2,1,720,128]{3,2,1,0:T(8,128)(2,1)S(1)}, u32[]{:S(2)}, u32[]{:S(2)}) collective-permute-start(bf16[2,1,720,128]{3,2,1,0:T(8,128)(2,1)S(1)} %get-tuple-element.5), channel_id=1, source_target_pairs={{0,8},{8,16},{16,24},{24,32},{32,40},{40,48},{48,56},{56,64},{64,7... | collective-permute-start | bytes 1105928 | tf_op jit(solution)/shard_map/ppermute | solution.py:16
  133.5 13.9 %collective-permute-start.5 = (bf16[2,1,720,128]{3,2,1,0:T(8,128)(2,1)S(1)}, bf16[2,1,720,128]{3,2,1,0:T(8,128)(2,1)S(1)}, u32[]{:S(2)}, u32[]{:S(2)}) collective-permute-start(bf16[2,1,720,128]{3,2,1,0:T(8,128)(2,1)S(1)} %get-tuple-element.6), channel_id=1, source_target_pairs={{8,0},{16,8},{24,16},{32,24},{40,32},{48,40},{56,48},{64,56},{72,6... | collective-permute-start | bytes 1105928 | tf_op jit(solution)/shard_map/ppermute | solution.py:17
  181.3 4.6 %copy-start.7 = (bf16[3,3,128,128]{3,2,1,0:T(8,128)(2,1)S(1)}, bf16[3,3,128,128]{3,2,1,0:T(8,128)(2,1)}, u32[]{:S(2)}) copy-start(bf16[3,3,128,128]{3,2,1,0:T(8,128)(2,1)} %param.14) | copy-start | bytes 884740
  181.3 4.6 %copy-start.9 = (pred[16,91]{0,1:T(8,128)(4,1)S(1)}, pred[16,91]{0,1:T(8,128)(4,1)}, u32[]{:S(2)}) copy-start(pred[16,91]{0,1:T(8,128)(4,1)} %constant.37) | copy-start | bytes 4372
  212.4 11.6 %copy-start.6 = (bf16[720,720]{1,0:T(8,128)(2,1)S(1)}, bf16[720,720]{1,0:T(8,128)(2,1)}, u32[]{:S(2)}) copy-start(bf16[720,720]{1,0:T(8,128)(2,1)} %param.15) | copy-start | bytes 3110404
  223.9 12.3 %copy-start.1 = (bf16[3,3,256,256]{3,2,1,0:T(8,128)(2,1)S(1)}, bf16[3,3,256,256]{3,2,1,0:T(8,128)(2,1)}, u32[]{:S(2)}) copy-start(bf16[3,3,256,256]{3,2,1,0:T(8,128)(2,1)} %param.9) | copy-start | bytes 3538948
